TPU v7x, 32 devices: a whole 2x2x4 slice. The times are simulated.
32 devices in a mesh: gx: 8 (over z, x), gy: 4 (over y, core).
Axes of the slice: x: 2, y: 2, z: 4, core: 2. Of those that a mesh axis runs over, the one named last changes fastest.
Arguments:
- source: float32 [128, 64, 256], P('gx', 'gy'), may hold values from -8 to 8
- conductivity: float32 [128, 64, 256], P('gx', 'gy'), may hold values from 0.25 to 8
- reaction: float32 [128, 64, 256], P('gx', 'gy'), may hold values from 0.02 to 0.2
Outputs:
- solution: float32 [128, 64, 256], P('gx', 'gy')
All inputs are finite; a program needn't handle non-finite values.
Results may differ from a plain program's by a relative error of at most 0.0003.
Values sent between devices are 32-bit elements; how exact they have to be, the bound alone decides.
A program may use at most 128 MiB of HBM per device.

v0:
```python
import functools

import jax
import jax.numpy as jnp
from jax import lax
from jax.experimental import pallas as pl
from jax.experimental.pallas import tpu as pltpu
from jax.sharding import PartitionSpec as P

DEGREE = 4
BOTTOM = 8
SMOOTH_LOWER = 0.5
SMOOTH_UPPER = 2.0
BOTTOM_LOWER = 0.02

MESH = pl.DeviceIdType.MESH
F32 = jnp.float32
H = 4
DIRS = [(dx, dy) for dx in (-1, 0, 1) for dy in (-1, 0, 1) if (dx, dy) != (0, 0)]


def steps(lower, upper, count):
    center, half = 0.5 * (upper + lower), 0.5 * (upper - lower)
    q = center / half
    p = 1.0 / q
    out = [(0.0, 1.0 / center)]
    for _ in range(1, count):
        pn = 1.0 / (2.0 * q - p)
        out.append((pn * p, 2.0 * pn / half))
        p = pn
    return out


def loop(lo, hi, body, unroll=1):
    def step(i, carry):
        body(i)
        return carry

    lax.fori_loop(lo, hi, step, 0, unroll=unroll)


def split_dot(v, m):
    hi = v.astype(jnp.bfloat16)
    lo = (v - hi.astype(F32)).astype(jnp.bfloat16)
    return jnp.dot(hi, m, preferred_element_type=F32) + jnp.dot(lo, m, preferred_element_type=F32)


def down_matrix(n):
    row = lax.broadcasted_iota(jnp.int32, (n, 128), 0)
    col = lax.broadcasted_iota(jnp.int32, (n, 128), 1)
    return jnp.where((row >= 2 * col) & (row < 2 * col + 2), 0.125, 0.0).astype(jnp.bfloat16)


def up_matrix(n):
    row = lax.broadcasted_iota(jnp.int32, (128, n), 0)
    col = lax.broadcasted_iota(jnp.int32, (128, n), 1)
    return jnp.where((col >= 2 * row) & (col < 2 * row + 2), 1.0, 0.0).astype(jnp.bfloat16)


class Level:
    def __init__(self, number, refs):
        self.s = 0.25**number
        self.f, self.b, self.c, self.x0, self.x1, self.d, self.g, self.inv, self.diag, self.w = refs
        self.nx, self.ny, self.nz = self.f.shape

    def zero(self, *refs):
        z = jnp.zeros((self.ny, self.nz), F32)

        def body(i):
            for r in refs:
                r[i] = z

        loop(0, self.nx, body)

    def setup(self, lo, hi):
        ny, nz = self.ny, self.nz
        row = lax.broadcasted_iota(jnp.int32, (ny, nz), 0)
        col = lax.broadcasted_iota(jnp.int32, (ny, nz), 1)
        edges = (row == 0, row == ny - 1, col == 0, col == nz - 1)

        def body(i):
            b = self.b[i]
            c = self.c[i]
            near = [
                self.b[i - 1],
                self.b[i + 1],
                jnp.where(edges[0], 0.0, pltpu.roll(b, 1, 0)),
                jnp.where(edges[1], 0.0, pltpu.roll(b, ny - 1, 0)),
                jnp.where(edges[2], 0.0, pltpu.roll(b, 1, 1)),
                jnp.where(edges[3], 0.0, pltpu.roll(b, nz - 1, 1)),
            ]
            half = 0.5 * self.s
            faces = [half * (b + n) for n in near]
            diag = c
            for face in faces:
                diag = diag + face
            inside = c > 0.0
            inv = jnp.where(inside, 1.0 / jnp.where(inside, diag, 1.0), 0.0)
            self.inv[i] = inv
            self.diag[i] = diag
            for k, face in enumerate(faces):
                w = face * inv
                if k >= 2:
                    w = jnp.where(edges[k - 2], 0.0, w)
                self.w[k, i] = w

        loop(lo, hi, body)

    def start(self, lo, hi, b):
        def body(i):
            g = self.f[i] * self.inv[i]
            self.g[i] = g
            d = g * b
            self.d[i] = d
            self.x0[i] = d

        loop(lo, hi, body)

    def scale_source(self, lo, hi):
        def body(i):
            self.g[i] = self.f[i] * self.inv[i]

        loop(lo, hi, body)

    def scaled_residual(self, x, i):
        v = x[i]
        t = self.g[i] - v
        t = t + self.w[0, i] * x[i - 1] + self.w[1, i] * x[i + 1]
        t = t + self.w[2, i] * pltpu.roll(v, 1, 0) + self.w[3, i] * pltpu.roll(v, self.ny - 1, 0)
        t = t + self.w[4, i] * pltpu.roll(v, 1, 1) + self.w[5, i] * pltpu.roll(v, self.nz - 1, 1)
        return v, t

    def sweep(self, x, y, a, b, lo, hi):
        def body(i):
            v, t = self.scaled_residual(x, i)
            d = b * t
            if a != 0.0:
                d = a * self.d[i] + d
            self.d[i] = d
            y[i] = v + d

        loop(lo, hi, body)

    def pre(self, lo, hi, shrink, pairs):
        self.start(lo, hi, pairs[0][1])
        x, y = self.x0, self.x1
        for a, b in pairs[1:]:
            lo, hi = lo + shrink, hi - shrink
            self.sweep(x, y, a, b, lo, hi)
            x, y = y, x
        return x, y

    def post(self, x, y, lo, hi, shrink, pairs):
        for a, b in pairs:
            lo, hi = lo + shrink, hi - shrink
            self.sweep(x, y, a, b, lo, hi)
            x, y = y, x
        return x, y

    def coarse_residual(self, x, first, count, m, scratch):
        def body(i):
            j = first + 2 * i
            _, t0 = self.scaled_residual(x, j)
            _, t1 = self.scaled_residual(x, j + 1)
            v = self.diag[j] * t0 + self.diag[j + 1] * t1
            scratch[i * self.ny : (i + 1) * self.ny, :] = split_dot(v, m)

        for i in range(count):
            body(i)


def coarse_array(ref, first, count, m, scratch):
    ny = ref.shape[1]
    for i in range(count):
        v = ref[first + 2 * i] + ref[first + 2 * i + 1]
        scratch[i * ny : (i + 1) * ny, :] = split_dot(v, m)


def pairs_of(scratch, start, size):
    return scratch[pl.ds(start, size, stride=2), :] + scratch[pl.ds(start + 1, size, stride=2), :]


def kernel(
    nx_dev, ny_dev, f_in, b_in, c_in, out, *refs
):
    refs = list(refs)

    def take(n):
        got = refs[:n]
        del refs[:n]
        return got

    levels = [Level(k, take(10)) for k in range(5)]
    l0, l1, l2, l3, l4 = levels
    scratch, e2pad, f2s, bc2s, f2l, bc2l = take(6)
    sx, sy, sc, rx, ry, rc = take(6)
    tx, ty, tc, ux, uy, uc = take(6)
    bc1s, bc1r, f1s, f1r, x1s, x1r = take(6)
    ssem, rsem, gssem, grsem = take(4)

    gx = lax.axis_index("gx")
    gy = lax.axis_index("gy")
    n = nx_dev * ny_dev
    me = gx * ny_dev + gy
    m256, m128 = down_matrix(256), down_matrix(128)
    u256, u128 = up_matrix(256), up_matrix(128)

    barrier = pltpu.get_barrier_semaphore()

    def greet(k):
        t = lax.rem(me + k, n)
        pl.semaphore_signal(
            barrier, inc=1, device_id=(t // ny_dev, lax.rem(t, ny_dev)), device_id_type=MESH
        )

    loop(1, n, greet)

    def present(dx, dy):
        ok = None
        for delta, at, size in ((dx, gx, nx_dev), (dy, gy, ny_dev)):
            if delta == 1:
                cond = at < size - 1
            elif delta == -1:
                cond = at > 0
            else:
                continue
            ok = cond if ok is None else ok & cond
        return ok

    def neighbour_copy(k, turn, src, dst):
        dx, dy = DIRS[k]
        return pltpu.make_async_remote_copy(
            src_ref=src,
            dst_ref=dst,
            send_sem=ssem.at[turn, k],
            recv_sem=rsem.at[turn, k],
            device_id=(gx + dx, gy + dy),
            device_id_type=MESH,
        )

    def slot(k, xs, ys, cs):
        dx, dy = DIRS[k]
        if dy == 0:
            return xs.at[(dx + 1) // 2]
        if dx == 0:
            return ys.at[(dy + 1) // 2]
        return cs.at[(dx + 1) + (dy + 1) // 2]

    def send_all(turn, pair_of):
        for k, (dx, dy) in enumerate(DIRS):

            @pl.when(present(dx, dy))
            def _():
                neighbour_copy(k, turn, *pair_of(k)).start()

    def arrive_all(turn, pair_of, use):
        for k, (dx, dy) in enumerate(DIRS):

            @pl.when(present(-dx, -dy))
            def _():
                neighbour_copy(k, turn, *pair_of(k)).wait_recv()
                use(k, dx, dy)

    def sent_all(turn, pair_of):
        for k, (dx, dy) in enumerate(DIRS):

            @pl.when(present(dx, dy))
            def _():
                neighbour_copy(k, turn, *pair_of(k)).wait_send()

    def source_span(delta):
        if delta == 0:
            return 0, 16, None, None
        return (16 - H, H, 16 - H, 15 - H) if delta == 1 else (0, H, H - 1, H)

    def landing(delta):
        return {0: (H, 16), 1: (0, H), -1: (H + 16, H)}[delta]

    for k, (dx, dy) in enumerate(DIRS):
        buf = slot(k, sx, sy, sc)
        px, cx, ox, beyx = source_span(dx)
        py, cy, oy, beyy = source_span(dy)
        for which, ref in enumerate((f_in, b_in, c_in)):

            def body(i, which=which, ref=ref, buf=buf, px=px, py=py, cy=cy):
                buf[which, i] = ref[px + i, py : py + cy, :]

            loop(0, cx, body)
        if dx != 0:
            i = ox - px
            buf[2, i] = buf[2, i] + 0.5 * b_in[beyx, py : py + cy, :]
        if dy != 0:

            def edge(i, buf=buf, px=px, py=py, oy=oy, beyy=beyy):
                buf[2, i, oy - py : oy - py + 1, :] = (
                    buf[2, i, oy - py : oy - py + 1, :] + 0.5 * b_in[px + i, beyy : beyy + 1, :]
                )

            loop(0, cx, edge)

    bc1 = []
    for which, ref in enumerate((b_in, c_in)):
        coarse_array(ref, 0, 8, m256, scratch)
        for i in range(8):
            bc1s[which, i] = pairs_of(scratch, 16 * i, 8)
    half = []
    for which in range(2):
        coarse_array(bc1s.at[which], 0, 4, m128, scratch)
        half.append(
            jnp.concatenate([pairs_of(scratch, 8 * i, 4) for i in range(4)], axis=0)
        )
    bc2s[...] = half[0] + pltpu.roll(half[1], 64, 1)

    pl.semaphore_wait(barrier, n - 1)

    strips = lambda k: (slot(k, sx, sy, sc), slot(k, rx, ry, rc))
    bricks = lambda s, r: (lambda k: (s, r.at[k]))
    send_all(0, strips)
    send_all(1, bricks(bc1s, bc1r))

    def gather_start(turn, src, dst):
        dst[me] = src[...]

        def body(k):
            t = lax.rem(me + k, n)
            pltpu.make_async_remote_copy(
                src_ref=src,
                dst_ref=dst.at[me],
                send_sem=gssem.at[turn],
                recv_sem=grsem.at[turn],
                device_id=(t // ny_dev, lax.rem(t, ny_dev)),
                device_id_type=MESH,
            ).start()

        loop(1, n, body)

    def gather_wait(turn, dst):
        whole = dst.at[pl.ds(0, n - 1)]
        other = lax.rem(me + 1, n)
        copy = pltpu.make_async_remote_copy(
            src_ref=whole,
            dst_ref=whole,
            send_sem=gssem.at[turn],
            recv_sem=grsem.at[turn],
            device_id=(other // ny_dev, lax.rem(other, ny_dev)),
            device_id_type=MESH,
        )
        copy.wait_send()
        copy.wait_recv()

    gather_start(0, bc2s, bc2l)

    l0.zero(l0.f, l0.b, l0.c)

    def inner(i):
        for dst, src in ((l0.f, f_in), (l0.b, b_in), (l0.c, c_in)):
            dst[i + 1 + H, H : H + 16, :] = src[i]

    loop(0, 16, inner)

    def place(dsts, xs, ys, cs):
        def use(k, dx, dy):
            buf = slot(k, xs, ys, cs)
            px, cx = landing(dx)
            py, cy = landing(dy)

            def body(i):
                for which, dst in enumerate(dsts):
                    dst[1 + px + i, py : py + cy, :] = buf[which, i]

            loop(0, cx, body)

        return use

    arrive_all(0, strips, place((l0.f, l0.b, l0.c), rx, ry, rc))
    l0.setup(1, 25)
    x0, y0 = l0.pre(1, 25, 1, steps(SMOOTH_LOWER, SMOOTH_UPPER, DEGREE))
    l0.coarse_residual(x0, 1 + H, 8, m256, scratch)
    for i in range(8):
        f1s[i] = pairs_of(scratch, 24 * i + H, 8)
    send_all(2, bricks(f1s, f1r))

    for k, (dx, dy) in enumerate(DIRS):
        buf = slot(k, tx, ty, tc)
        px, cx, _, _ = source_span(dx)
        py, cy, _, _ = source_span(dy)

        def body(i, buf=buf, px=px, py=py, cy=cy):
            buf[0, i] = x0[1 + H + px + i, H + py : H + py + cy, :]

        loop(0, cx, body)
    xstrips = lambda k: (slot(k, tx, ty, tc), slot(k, ux, uy, uc))

    l1.zero(l1.f, l1.b, l1.c)

    def brick(dsts, src):
        def use(k, dx, dy):
            for which, dst in enumerate(dsts):
                for i in range(8):
                    dst[9 - 8 * dx + i, 8 - 8 * dy : 16 - 8 * dy, :] = src(k, which, i)

        return use

    for i in range(8):
        l1.b[9 + i, 8:16, :] = bc1s[0, i]
        l1.c[9 + i, 8:16, :] = bc1s[1, i]
        l1.f[9 + i, 8:16, :] = f1s[i]
    arrive_all(1, bricks(bc1s, bc1r), brick((l1.b, l1.c), lambda k, w, i: bc1r[k, w, i]))
    l1.setup(1, 25)
    arrive_all(2, bricks(f1s, f1r), brick((l1.f,), lambda k, w, i: f1r[k, i]))
    x1, y1 = l1.pre(1, 25, 1, steps(SMOOTH_LOWER, SMOOTH_UPPER, DEGREE))
    l1.coarse_residual(x1, 9, 4, m128, scratch)
    f2 = [pairs_of(scratch, 24 * i + 8, 4) for i in range(4)]
    f2s[...] = jnp.concatenate(f2[:2], axis=0) + pltpu.roll(
        jnp.concatenate(f2[2:], axis=0), 64, 1
    )
    gather_start(1, f2s, f2l)
    for i in range(8):
        x1s[i] = x1[9 + i, 8:16, :]
    send_all(3, bricks(x1s, x1r))
    send_all(4, xstrips)

    for lv in (l2, l3, l4):
        lv.zero(lv.f, lv.b, lv.c, lv.x0, lv.x1)
    gather_wait(0, bc2l)

    def low(v):
        col = lax.broadcasted_iota(jnp.int32, v.shape, 1)
        return jnp.where(col < 64, v, 0.0)

    def spread_bc(a):
        for e in range(ny_dev):
            v = bc2l[a * ny_dev + e]
            b2, c2 = low(v), low(pltpu.roll(v, 64, 1))
            for i in range(4):
                l2.b[1 + 4 * a + i, 4 * e : 4 * e + 4, :] = b2[4 * i : 4 * i + 4]
                l2.c[1 + 4 * a + i, 4 * e : 4 * e + 4, :] = c2[4 * i : 4 * i + 4]

    loop(0, nx_dev, spread_bc)
    for fine, coarse in ((l2, l3), (l3, l4)):
        nxc, nyc = (fine.nx - 2) // 2, fine.ny // 2
        for src, dst in ((fine.b, coarse.b), (fine.c, coarse.c)):
            coarse_array(src, 1, nxc, m128, scratch)
            for i in range(nxc):
                dst[1 + i, 0:nyc, :] = pairs_of(scratch, fine.ny * i, nyc)
    for lv in (l2, l3, l4):
        lv.setup(1, lv.nx - 1)

    gather_wait(1, f2l)

    def spread_f(a):
        for e in range(ny_dev):
            v = f2l[a * ny_dev + e]
            p01, p23 = low(v), low(pltpu.roll(v, 64, 1))
            for i in range(4):
                p = (p01, p23)[i // 2]
                r = 4 * (i % 2)
                l2.f[1 + 4 * a + i, 4 * e : 4 * e + 4, :] = p[r : r + 4]

    loop(0, nx_dev, spread_f)
    found = []
    for fine, coarse in ((l2, l3), (l3, l4)):
        x, y = fine.pre(1, fine.nx - 1, 0, steps(SMOOTH_LOWER, SMOOTH_UPPER, DEGREE))
        found.append((x, y))
        nxc, nyc = (fine.nx - 2) // 2, fine.ny // 2
        fine.coarse_residual(x, 1, nxc, m128, scratch)
        for i in range(nxc):
            coarse.f[1 + i, 0:nyc, :] = pairs_of(scratch, fine.ny * i, nyc)
    e, _ = l4.pre(1, l4.nx - 1, 0, steps(BOTTOM_LOWER, SMOOTH_UPPER, BOTTOM))

    def refine_plane(v, rows, at, u):
        scratch[pl.ds(at, rows, stride=2), :] = v
        scratch[pl.ds(at + 1, rows, stride=2), :] = v
        return split_dot(scratch[at : at + 2 * rows, :], u)

    for fine, coarse, (x, y) in ((l3, l4, found[1]), (l2, l3, found[0])):
        nxc, nyc = (fine.nx - 2) // 2, fine.ny // 2
        for i in range(nxc):
            up = refine_plane(e[1 + i][0:nyc], nyc, i * fine.ny, u128)
            x[1 + 2 * i] = x[1 + 2 * i] + up
            x[2 + 2 * i] = x[2 + 2 * i] + up
        e, _ = fine.post(x, y, 1, fine.nx - 1, 0, steps(SMOOTH_LOWER, SMOOTH_UPPER, DEGREE))

    yt = e2pad.shape[1]
    zero_plane = jnp.zeros((yt, 128), F32)

    def clear(i):
        e2pad[i] = zero_plane

    loop(0, e2pad.shape[0], clear)

    def pad_e2(i):
        e2pad[4 + i, 4 : 4 + l2.ny, :] = e[1 + i]

    loop(0, l2.nx - 2, pad_e2)
    arrive_all(3, bricks(x1s, x1r), brick((x1,), lambda k, w, i: x1r[k, i]))

    def add(fine, x, j, up):
        x[j] = jnp.where(fine.inv[j] > 0.0, x[j] + up, 0.0)

    turn_by = lax.rem(yt - 4 * gy, yt)
    for i in range(12):
        v = pltpu.roll(e2pad[4 * gx + i], turn_by, 0)[0:12]
        up = refine_plane(v, 12, 24 * i, u128)
        add(l1, x1, 1 + 2 * i, up)
        add(l1, x1, 2 + 2 * i, up)
    e1, _ = l1.post(x1, y1, 3, 23, 1, steps(SMOOTH_LOWER, SMOOTH_UPPER, DEGREE))

    arrive_all(4, xstrips, place((x0,), ux, uy, uc))
    for i in range(12):
        up = refine_plane(e1[7 + i][6:18], 12, 24 * i, u256)
        add(l0, x0, 1 + 2 * i, up)
        add(l0, x0, 2 + 2 * i, up)
    r0, _ = l0.post(x0, y0, 1, 25, 1, steps(SMOOTH_LOWER, SMOOTH_UPPER, DEGREE))

    def give(i):
        out[i] = r0[1 + H + i, H : H + 16, :]

    loop(0, 16, give)
    sent_all(0, strips)
    sent_all(1, bricks(bc1s, bc1r))
    sent_all(2, bricks(f1s, f1r))
    sent_all(3, bricks(x1s, x1r))
    sent_all(4, xstrips)


def solution(mesh):
    nx_dev, ny_dev = mesh.shape["gx"], mesh.shape["gy"]
    n = nx_dev * ny_dev
    y2 = 4 * ny_dev

    def vm(*shape):
        return pltpu.VMEM(shape, F32)

    dims = [(26, 24, 256), (26, 24, 128)]
    for k in range(3):
        dims.append((2 + (4 * nx_dev >> k), max(8, y2 >> k), 128))
    shapes = []
    for d in dims:
        shapes += [vm(*d)] * 9 + [vm(6, *d)]
    shapes += [
        vm(max(12 * 24, 2 * nx_dev * y2), 128),
        vm(4 * nx_dev + 8, y2 + 8, 128),
        vm(8, 128),
        vm(16, 128),
        vm(n, 8, 128),
        vm(n, 16, 128),
    ]
    for count in (3, 3, 1, 1):
        shapes += [
            vm(2, count, H, 16, 256),
            vm(2, count, 16, H, 256),
            vm(4, count, H, H, 256),
        ]
    shapes += [vm(2, 8, 8, 128), vm(8, 2, 8, 8, 128)]
    shapes += [vm(8, 8, 128), vm(8, 8, 8, 128)] * 2
    shapes += [
        pltpu.SemaphoreType.DMA((5, 8)),
        pltpu.SemaphoreType.DMA((5, 8)),
        pltpu.SemaphoreType.DMA((2,)),
        pltpu.SemaphoreType.DMA((2,)),
    ]

    def per_device(source, conductivity, reaction):
        return pl.pallas_call(
            functools.partial(kernel, nx_dev, ny_dev),
            out_shape=jax.ShapeDtypeStruct(source.shape, F32),
            in_specs=[pl.BlockSpec(memory_space=pltpu.VMEM)] * 3,
            out_specs=pl.BlockSpec(memory_space=pltpu.VMEM),
            scratch_shapes=shapes,
            compiler_params=pltpu.CompilerParams(
                collective_id=0, has_side_effects=True, vmem_limit_bytes=48 << 20
            ),
        )(source, conductivity, reaction)

    spec = P("gx", "gy", None)
    return jax.shard_map(
        per_device, mesh=mesh, in_specs=(spec,) * 3, out_specs=spec, check_vma=False
    )
```

profile of v0, /device:TPU:9, one launch (start us, length us, event | category | flops | bytes accessed | tf_op | source)
XLA Modules:
  0.0 101.9 jit_solution(12396013642029271692)
XLA Ops:
  0.0 0.0 copy-start
  0.0 0.9 copy-done
  1.0 0.0 copy-start.1
  1.0 0.9 copy-done.1
  1.9 0.0 copy-start.2
  1.9 0.9 copy-done.2
  2.9 98.4 %shard_map.37 = f32[16,16,256]{2,1,0:T(8,128)S(1)} custom-call(f32[16,16,256]{2,1,0:T(8,128)S(1)} %copy-done, f32[16,16,256]{2,1,0:T(8,128)S(1)} %copy-done.1, f32[16,16,256]{2,1,0:T(8,128)S(1)} %copy-done.2), custom_call_target="tpu_custom_call" | custom-call | tf_op jit(solution)/shard_map/pallas_call | solution.py:565
  101.2 0.7 copy.5
Async XLA Ops:
  0.0 0.9 copy-start
  1.0 0.9 copy-start.1
  1.9 0.9 copy-start.2
where the time goes:
time: 102 us
  Pallas kernels  98.4 us (96%)
  local copies, waits for them, and re-layouts  3.55 us (3%)
    pallas_call x1, Pallas kernels, per_device(): pl.pallas_call(functools.partial(kernel, nx_dev, ny_dev), out_shape=jax.S...  98.4 us
    unnamed x7, local copies, waits for them, and re-layouts  3.55 us

commit v1 on v0

--- a/solution.py
+++ b/solution.py
@@ -39,6 +39,25 @@
     lax.fori_loop(lo, hi, step, 0, unroll=unroll)
 
 
+def planes(lo, hi, body, chunk):
+    chunk = min(chunk, hi - lo)
+
+    def group(i, size):
+        stores = []
+        for k in range(size):
+            stores += body(i + k)
+        for ref, index, value in stores:
+            ref[index] = value
+
+    whole = (hi - lo) // chunk
+    if whole == 1:
+        group(lo, chunk)
+    else:
+        loop(0, whole, lambda j: group(lo + j * chunk, chunk))
+    if whole * chunk < hi - lo:
+        group(lo + whole * chunk, hi - lo - whole * chunk)
+
+
 def split_dot(v, m):
     hi = v.astype(jnp.bfloat16)
     lo = (v - hi.astype(F32)).astype(jnp.bfloat16)
@@ -62,15 +81,13 @@
         self.s = 0.25**number
         self.f, self.b, self.c, self.x0, self.x1, self.d, self.g, self.inv, self.diag, self.w = refs
         self.nx, self.ny, self.nz = self.f.shape
+        vregs = self.ny * self.nz // 1024
+        self.chunk = max(2, 16 // vregs)
 
     def zero(self, *refs):
         z = jnp.zeros((self.ny, self.nz), F32)
 
-        def body(i):
-            for r in refs:
-                r[i] = z
-
-        loop(0, self.nx, body)
+        planes(0, self.nx, lambda i: [(r, i, z) for r in refs], self.chunk)
 
     def setup(self, lo, hi):
         ny, nz = self.ny, self.nz
@@ -96,31 +113,23 @@
                 diag = diag + face
             inside = c > 0.0
             inv = jnp.where(inside, 1.0 / jnp.where(inside, diag, 1.0), 0.0)
-            self.inv[i] = inv
-            self.diag[i] = diag
+            stores = [(self.inv, i, inv), (self.diag, i, diag)]
             for k, face in enumerate(faces):
                 w = face * inv
                 if k >= 2:
                     w = jnp.where(edges[k - 2], 0.0, w)
-                self.w[k, i] = w
-
-        loop(lo, hi, body)
+                stores.append((self.w, (k, i), w))
+            return stores
+
+        planes(lo, hi, body, self.chunk)
 
     def start(self, lo, hi, b):
         def body(i):
             g = self.f[i] * self.inv[i]
-            self.g[i] = g
             d = g * b
-            self.d[i] = d
-            self.x0[i] = d
-
-        loop(lo, hi, body)
-
-    def scale_source(self, lo, hi):
-        def body(i):
-            self.g[i] = self.f[i] * self.inv[i]
-
-        loop(lo, hi, body)
+            return [(self.g, i, g), (self.d, i, d), (self.x0, i, d)]
+
+        planes(lo, hi, body, self.chunk)
 
     def scaled_residual(self, x, i):
         v = x[i]
@@ -136,10 +145,9 @@
             d = b * t
             if a != 0.0:
                 d = a * self.d[i] + d
-            self.d[i] = d
-            y[i] = v + d
-
-        loop(lo, hi, body)
+            return [(self.d, i, d), (y, i, v + d)]
+
+        planes(lo, hi, body, self.chunk)
 
     def pre(self, lo, hi, shrink, pairs):
         self.start(lo, hi, pairs[0][1])

time: 102 us -> 61.4 us (0.60)
  Pallas kernels: 98.4 us -> 57.6 us
    pallas_call x1, Pallas kernels: 98.4 us -> 57.6 us  [per_device(): pl.pallas_call(functools.partial(kernel, nx_dev, ny_dev), out_shape=jax.S...]
where the time goes in v1:
time: 61.4 us; the launch traced here: 61.2 us
  Pallas kernels  57.6 us (94%)
  local copies, waits for them, and re-layouts  3.55 us (6%)
    pallas_call x1, Pallas kernels, per_device(): pl.pallas_call(functools.partial(kernel, nx_dev, ny_dev), out_shape=jax.S...  57.6 us
    unnamed x7, local copies, waits for them, and re-layouts  3.55 us

profile of v1, /device:TPU:9, one launch (start us, length us, event | category | flops | bytes accessed | tf_op | source)
XLA Modules:
  0.0 61.2 jit_solution(12812905760083087586)
XLA Ops:
  0.0 0.0 copy-start
  0.0 0.9 %copy-done = f32[16,16,256]{2,1,0:T(8,128)S(1)} copy-done((f32[16,16,256]{2,1,0:T(8,128)S(1)}, f32[16,16,256]{2,1,0:T(8,128)}, u32[]{:S(2)}) %copy-start) | copy-done | bytes 262168
  1.0 0.0 copy-start.1
  1.0 0.9 %copy-done.1 = f32[16,16,256]{2,1,0:T(8,128)S(1)} copy-done((f32[16,16,256]{2,1,0:T(8,128)S(1)}, f32[16,16,256]{2,1,0:T(8,128)}, u32[]{:S(2)}) %copy-start.1) | copy-done | bytes 262168
  1.9 0.0 copy-start.2
  1.9 0.9 %copy-done.2 = f32[16,16,256]{2,1,0:T(8,128)S(1)} copy-done((f32[16,16,256]{2,1,0:T(8,128)S(1)}, f32[16,16,256]{2,1,0:T(8,128)}, u32[]{:S(2)}) %copy-start.2) | copy-done | bytes 262168
  2.9 57.6 %shard_map.37 = f32[16,16,256]{2,1,0:T(8,128)S(1)} custom-call(f32[16,16,256]{2,1,0:T(8,128)S(1)} %copy-done, f32[16,16,256]{2,1,0:T(8,128)S(1)} %copy-done.1, f32[16,16,256]{2,1,0:T(8,128)S(1)} %copy-done.2), custom_call_target="tpu_custom_call" | custom-call | tf_op jit(solution)/shard_map/pallas_call | solution.py:573
  60.5 0.7 %copy.5 = f32[16,16,256]{2,1,0:T(8,128)} copy(f32[16,16,256]{2,1,0:T(8,128)S(1)} %shard_map.37) | data formatting | bytes 524288
Async XLA Ops:
  0.0 0.9 %copy-start = (f32[16,16,256]{2,1,0:T(8,128)S(1)}, f32[16,16,256]{2,1,0:T(8,128)}, u32[]{:S(2)}) copy-start(f32[16,16,256]{2,1,0:T(8,128)} %f_in.1) | copy-start | bytes 786436
  1.0 0.9 %copy-start.1 = (f32[16,16,256]{2,1,0:T(8,128)S(1)}, f32[16,16,256]{2,1,0:T(8,128)}, u32[]{:S(2)}) copy-start(f32[16,16,256]{2,1,0:T(8,128)} %b_in.1) | copy-start | bytes 786436
  1.9 0.9 %copy-start.2 = (f32[16,16,256]{2,1,0:T(8,128)S(1)}, f32[16,16,256]{2,1,0:T(8,128)}, u32[]{:S(2)}) copy-start(f32[16,16,256]{2,1,0:T(8,128)} %c_in.1) | copy-start | bytes 786436

commit v2 on v1

--- a/solution.py
+++ b/solution.py
@@ -17,6 +17,7 @@
 F32 = jnp.float32
 H = 4
 DIRS = [(dx, dy) for dx in (-1, 0, 1) for dy in (-1, 0, 1) if (dx, dy) != (0, 0)]
+DIRS.sort(key=lambda way: way[0] == 0)
 
 
 def steps(lower, upper, count):
@@ -261,8 +262,10 @@
             def _():
                 neighbour_copy(k, turn, *pair_of(k)).start()
 
-    def arrive_all(turn, pair_of, use):
+    def arrive_all(turn, pair_of, use, want=lambda dx: True):
         for k, (dx, dy) in enumerate(DIRS):
+            if not want(dx):
+                continue
 
             @pl.when(present(-dx, -dy))
             def _():
@@ -291,9 +294,9 @@
         for which, ref in enumerate((f_in, b_in, c_in)):
 
             def body(i, which=which, ref=ref, buf=buf, px=px, py=py, cy=cy):
-                buf[which, i] = ref[px + i, py : py + cy, :]
-
-            loop(0, cx, body)
+                return [(buf, (which, i), ref[px + i, py : py + cy, :])]
+
+            planes(0, cx, body, 4)
         if dx != 0:
             i = ox - px
             buf[2, i] = buf[2, i] + 0.5 * b_in[beyx, py : py + cy, :]
@@ -305,6 +308,12 @@
                 )
 
             loop(0, cx, edge)
+
+    pl.semaphore_wait(barrier, n - 1)
+
+    strips = lambda k: (slot(k, sx, sy, sc), slot(k, rx, ry, rc))
+    bricks = lambda s, r: (lambda k: (s, r.at[k]))
+    send_all(0, strips)
 
     bc1 = []
     for which, ref in enumerate((b_in, c_in)):
@@ -318,13 +327,6 @@
             jnp.concatenate([pairs_of(scratch, 8 * i, 4) for i in range(4)], axis=0)
         )
     bc2s[...] = half[0] + pltpu.roll(half[1], 64, 1)
-
-    pl.semaphore_wait(barrier, n - 1)
-
-    strips = lambda k: (slot(k, sx, sy, sc), slot(k, rx, ry, rc))
-    bricks = lambda s, r: (lambda k: (s, r.at[k]))
-    send_all(0, strips)
-    send_all(1, bricks(bc1s, bc1r))
 
     def gather_start(turn, src, dst):
         dst[me] = src[...]
@@ -356,15 +358,16 @@
         copy.wait_send()
         copy.wait_recv()
 
-    gather_start(0, bc2s, bc2l)
 
     l0.zero(l0.f, l0.b, l0.c)
 
     def inner(i):
-        for dst, src in ((l0.f, f_in), (l0.b, b_in), (l0.c, c_in)):
-            dst[i + 1 + H, H : H + 16, :] = src[i]
-
-    loop(0, 16, inner)
+        return [
+            (dst, (i + 1 + H, slice(H, H + 16)), src[i])
+            for dst, src in ((l0.f, f_in), (l0.b, b_in), (l0.c, c_in))
+        ]
+
+    planes(0, 16, inner, 2)
 
     def place(dsts, xs, ys, cs):
         def use(k, dx, dy):
@@ -373,16 +376,33 @@
             py, cy = landing(dy)
 
             def body(i):
-                for which, dst in enumerate(dsts):
-                    dst[1 + px + i, py : py + cy, :] = buf[which, i]
-
-            loop(0, cx, body)
+                return [
+                    (dst, (1 + px + i, slice(py, py + cy)), buf[which, i])
+                    for which, dst in enumerate(dsts)
+                ]
+
+            planes(0, cx, body, 4)
 
         return use
 
-    arrive_all(0, strips, place((l0.f, l0.b, l0.c), rx, ry, rc))
-    l0.setup(1, 25)
-    x0, y0 = l0.pre(1, 25, 1, steps(SMOOTH_LOWER, SMOOTH_UPPER, DEGREE))
+    landed = place((l0.f, l0.b, l0.c), rx, ry, rc)
+    arrive_all(0, strips, landed, lambda dx: dx == 0)
+    smoothing = steps(SMOOTH_LOWER, SMOOTH_UPPER, DEGREE)
+    l0.setup(6, 20)
+    x0, y0 = l0.pre(6, 20, 1, smoothing)
+    arrive_all(0, strips, landed, lambda dx: dx != 0)
+    send_all(1, bricks(bc1s, bc1r))
+    gather_start(0, bc2s, bc2l)
+    l0.setup(1, 6)
+    l0.setup(20, 25)
+    l0.start(1, 6, smoothing[0][1])
+    l0.start(20, 25, smoothing[0][1])
+    now, later = l0.x0, l0.x1
+    for k in range(1, DEGREE):
+        a, b = smoothing[k]
+        l0.sweep(now, later, a, b, 1 + k, 6 + k)
+        l0.sweep(now, later, a, b, 20 - k, 25 - k)
+        now, later = later, now
     l0.coarse_residual(x0, 1 + H, 8, m256, scratch)
     for i in range(8):
         f1s[i] = pairs_of(scratch, 24 * i + H, 8)
@@ -394,9 +414,9 @@
         py, cy, _, _ = source_span(dy)
 
         def body(i, buf=buf, px=px, py=py, cy=cy):
-            buf[0, i] = x0[1 + H + px + i, H + py : H + py + cy, :]
-
-        loop(0, cx, body)
+            return [(buf, (0, i), x0[1 + H + px + i, H + py : H + py + cy, :])]
+
+        planes(0, cx, body, 4)
     xstrips = lambda k: (slot(k, tx, ty, tc), slot(k, ux, uy, uc))
 
     l1.zero(l1.f, l1.b, l1.c)
@@ -522,9 +542,9 @@
     r0, _ = l0.post(x0, y0, 1, 25, 1, steps(SMOOTH_LOWER, SMOOTH_UPPER, DEGREE))
 
     def give(i):
-        out[i] = r0[1 + H + i, H : H + 16, :]
-
-    loop(0, 16, give)
+        return [(out, i, r0[1 + H + i, H : H + 16, :])]
+
+    planes(0, 16, give, 4)
     sent_all(0, strips)
     sent_all(1, bricks(bc1s, bc1r))
     sent_all(2, bricks(f1s, f1r))

time: 61.4 us -> 58.1 us (0.946)
  the two profiles are of different devices: /device:TPU:9 before, /device:TPU:0 now
where the time goes in v2:
time: 58.1 us; the launch traced here: 57.9 us
  Pallas kernels  54.4 us (94%)
  local copies, waits for them, and re-layouts  3.55 us (6%)
    pallas_call x1, Pallas kernels, per_device(): pl.pallas_call(functools.partial(kernel, nx_dev, ny_dev), out_shape=jax.S...  54.4 us
    unnamed x7, local copies, waits for them, and re-layouts  3.55 us

profile of v2, /device:TPU:0, one launch (start us, length us, event | category | flops | bytes accessed | tf_op | source)
XLA Modules:
  0.0 57.9 jit_solution(7466927109496703229)
XLA Ops:
  0.0 0.0 copy-start
  0.0 0.9 %copy-done = f32[16,16,256]{2,1,0:T(8,128)S(1)} copy-done((f32[16,16,256]{2,1,0:T(8,128)S(1)}, f32[16,16,256]{2,1,0:T(8,128)}, u32[]{:S(2)}) %copy-start) | copy-done | bytes 262168
  1.0 0.0 copy-start.1
  1.0 0.9 %copy-done.1 = f32[16,16,256]{2,1,0:T(8,128)S(1)} copy-done((f32[16,16,256]{2,1,0:T(8,128)S(1)}, f32[16,16,256]{2,1,0:T(8,128)}, u32[]{:S(2)}) %copy-start.1) | copy-done | bytes 262168
  1.9 0.0 copy-start.2
  1.9 0.9 %copy-done.2 = f32[16,16,256]{2,1,0:T(8,128)S(1)} copy-done((f32[16,16,256]{2,1,0:T(8,128)S(1)}, f32[16,16,256]{2,1,0:T(8,128)}, u32[]{:S(2)}) %copy-start.2) | copy-done | bytes 262168
  2.9 54.4 %shard_map.37 = f32[16,16,256]{2,1,0:T(8,128)S(1)} custom-call(f32[16,16,256]{2,1,0:T(8,128)S(1)} %copy-done, f32[16,16,256]{2,1,0:T(8,128)S(1)} %copy-done.1, f32[16,16,256]{2,1,0:T(8,128)S(1)} %copy-done.2), custom_call_target="tpu_custom_call" | custom-call | tf_op jit(solution)/shard_map/pallas_call | solution.py:593
  57.2 0.7 %copy.5 = f32[16,16,256]{2,1,0:T(8,128)} copy(f32[16,16,256]{2,1,0:T(8,128)S(1)} %shard_map.37) | data formatting | bytes 524288
Async XLA Ops:
  0.0 0.9 %copy-start = (f32[16,16,256]{2,1,0:T(8,128)S(1)}, f32[16,16,256]{2,1,0:T(8,128)}, u32[]{:S(2)}) copy-start(f32[16,16,256]{2,1,0:T(8,128)} %f_in.1) | copy-start | bytes 786436
  1.0 0.9 %copy-start.1 = (f32[16,16,256]{2,1,0:T(8,128)S(1)}, f32[16,16,256]{2,1,0:T(8,128)}, u32[]{:S(2)}) copy-start(f32[16,16,256]{2,1,0:T(8,128)} %b_in.1) | copy-start | bytes 786436
  1.9 0.9 %copy-start.2 = (f32[16,16,256]{2,1,0:T(8,128)S(1)}, f32[16,16,256]{2,1,0:T(8,128)}, u32[]{:S(2)}) copy-start(f32[16,16,256]{2,1,0:T(8,128)} %c_in.1) | copy-start | bytes 786436
